TPU v7x, 128 devices: a whole 4x4x4 slice. The times are simulated.
128 devices in a mesh: chan: 32 (over x, z_hi, y), grp: 4 (over z_lo, core).
Axes of the slice: x: 4, y: 4, z: 4 (z_hi: 2, z_lo: 2; z = z_hi * 2 + z_lo), core: 2. Of those that a mesh axis runs over, the one named last changes fastest.
Arguments:
- voltages: bfloat16 [512, 4096, 128], P(('chan', 'grp')), may hold values from -6 to 6
- delays: int32 [64, 512], replicated, may hold values from 0 to 4095
- shifts: int32 [256, 512], replicated, may hold values from 0 to 511
Outputs:
- dm_power: float32 [256, 512, 256], P('grp', 'chan')
All inputs are finite; a program needn't handle non-finite values.
Results may differ from a plain program's by a relative error of at most 0.011.
Values may be sent and summed in bfloat16 or wider, within the bound.
No kernel may reach another device: no remote copies, remote signals or barrier semaphores. Data moves between devices by JAX's collectives and lax.ppermute only.
A program may use at most 128 MiB of HBM per device.

v0:
```python
import math
import jax
import jax.numpy as jnp
from jax import lax
from jax.sharding import PartitionSpec as P

DISHES = 64
INTEG = 8
PHASES = 4096
KBLK = 16


def beam_matrix(delays, channel, channel_count):
    frequency = channel + channel_count
    residue = jnp.mod(delays * frequency, PHASES)
    phases = residue.astype(jnp.float32) * jnp.float32(2.0 * math.pi / PHASES)
    weight_scale = jnp.float32(1.0 / math.sqrt(DISHES))
    real_part = jnp.cos(phases) * weight_scale
    imag_part = -jnp.sin(phases) * weight_scale
    upper = jnp.concatenate([real_part, imag_part], axis=1)
    lower = jnp.concatenate([-imag_part, real_part], axis=1)
    return jnp.concatenate([upper, lower], axis=0).astype(jnp.bfloat16)


def detect(samples, matrix):
    beams = jnp.dot(samples, matrix, preferred_element_type=jnp.float32)
    half_width = matrix.shape[1] // 2
    intensity = beams[:, :half_width] ** 2 + beams[:, half_width:] ** 2
    steps_count = samples.shape[0] // INTEG
    averaged = jnp.sum(intensity.reshape(steps_count, INTEG, half_width), axis=1) * jnp.float32(
        1.0 / INTEG
    )
    return averaged.T.astype(jnp.bfloat16)


def dft_table(length):
    bins_count = length // 2
    sample_index = jnp.arange(length, dtype=jnp.int32)[:, None]
    freq_index = jnp.arange(1, bins_count + 1, dtype=jnp.int32)[None, :]
    residue = jnp.mod(sample_index * freq_index, length)
    phases = residue.astype(jnp.float32) * jnp.float32(2.0 * math.pi / length)
    norm_scale = jnp.float32(1.0 / math.sqrt(length))
    return jnp.concatenate(
        [jnp.cos(phases) * norm_scale, -jnp.sin(phases) * norm_scale], axis=1
    ).astype(jnp.bfloat16)


def spectra(series, table):
    flat = series.reshape(-1, series.shape[-1])
    result = jnp.dot(flat, table, preferred_element_type=jnp.float32).astype(jnp.bfloat16)
    return result.reshape(series.shape[:-1] + (table.shape[1],))


def dedisperse(spectrum, selected, phase_scale):
    channel_count, beam_count, doubled = spectrum.shape
    bins_count = doubled // 2
    trial_count = selected.shape[0]
    parted = spectrum.reshape(channel_count, beam_count, 2, bins_count).transpose(2, 3, 1, 0)
    real_spec = parted[0]
    imag_spec = parted[1]
    across = selected.T

    def one_block(block_index):
        start = block_index * KBLK
        real_piece = lax.dynamic_slice_in_dim(real_spec, start, KBLK, 0)
        imag_piece = lax.dynamic_slice_in_dim(imag_spec, start, KBLK, 0)
        freq_index = (start + jnp.arange(KBLK, dtype=jnp.int32) + 1)[:, None, None]
        residue = jnp.mod(freq_index * across[None, :, :], doubled)
        phases = residue.astype(jnp.float32) * jnp.float32(2.0 * math.pi / doubled)
        cosine = (jnp.cos(phases) * phase_scale).astype(jnp.bfloat16)
        sine = (jnp.sin(phases) * phase_scale).astype(jnp.bfloat16)
        cos_real = jnp.einsum(
            "kbc,kcm->kbm", real_piece, cosine, preferred_element_type=jnp.float32
        )
        sin_imag = jnp.einsum("kbc,kcm->kbm", imag_piece, sine, preferred_element_type=jnp.float32)
        sin_real = jnp.einsum("kbc,kcm->kbm", real_piece, sine, preferred_element_type=jnp.float32)
        cos_imag = jnp.einsum(
            "kbc,kcm->kbm", imag_piece, cosine, preferred_element_type=jnp.float32
        )
        return jnp.stack([cos_real - sin_imag, sin_real + cos_imag], axis=1)

    blocks = lax.map(one_block, jnp.arange(bins_count // KBLK, dtype=jnp.int32))
    return blocks.reshape(bins_count, 2, beam_count, trial_count)


def body(voltages, delays, shifts):
    chan_count = lax.axis_size("chan")
    group_count = lax.axis_size("grp")
    chan_local = voltages.shape[0]
    channel_total = chan_local * chan_count * group_count
    first_channel = (lax.axis_index("chan") * group_count + lax.axis_index("grp")) * chan_local

    def detect_channel(item):
        samples, offset = item
        return detect(samples, beam_matrix(delays, first_channel + offset, channel_total))

    detected = lax.map(detect_channel, (voltages, jnp.arange(chan_local, dtype=jnp.int32)))
    table = dft_table(detected.shape[2])
    phase_scale = jnp.float32(1.0 / math.sqrt(channel_total))
    trial_count = shifts.shape[0]
    grouped = shifts.reshape(trial_count, chan_count, group_count, chan_local)
    selected = lax.dynamic_index_in_dim(grouped, lax.axis_index("grp"), axis=2, keepdims=False)
    selected = selected.reshape(trial_count, chan_count * chan_local)
    beam_total = detected.shape[1]
    blocked = detected.reshape(chan_local, chan_count, beam_total // chan_count, detected.shape[2])
    partial_spec = dedisperse(
        spectra(
            lax.all_to_all(blocked, "chan", split_axis=1, concat_axis=0, tiled=True)[:, 0], table
        ),
        selected,
        phase_scale,
    )
    summed = lax.psum_scatter(partial_spec, "grp", scatter_dimension=3, tiled=True)
    result = summed[:, 0] ** 2 + summed[:, 1] ** 2
    return result.transpose(2, 1, 0)


def solution(mesh):
    placed = (P(("chan", "grp"), None, None), P(), P())
    return jax.shard_map(
        body, mesh=mesh, in_specs=placed, out_specs=P("grp", "chan", None), check_vma=False
    )
```

profile of v0, /device:TPU:1, one launch (start us, length us, event | category | flops | bytes accessed | tf_op | source)
XLA Modules:
  0.0 781.8 jit_solution(4878138713700647623)
XLA Ops:
  6.5 39.4 %while.24 = (s32[]{:T(128)}, bf16[4,512,512]{2,1,0:T(8,128)(2,1)S(1)}, bf16[4,4096,128]{2,1,0:T(8,128)(2,1)}, s32[4]{0:T(128)S(1)}, s32[]{:T(128)}, /*index=5*/s32[64,512]{1,0:T(8,128)}, s32[]{:T(128)}, s32[]{:T(128)}) while((s32[]{:T(128)}, bf16[4,512,512]{2,1,0:T(8,128)(2,1)S(1)}, bf16[4,4096,128]{2,1,0:T(8,128)(2,1)}, s32[4]{0:T(128)S(1)}, ...), condition=%wide.region_2.3_spmd, body=%wide.region_0.2_spmd.sunk | while | flops 1084129280 | bytes 39846528 | solution.py:97
  47.6 11.3 %all-to-all-start = ((bf16[4,32,16,512]{3,2,0,1:T(8,128)(2,1)}), bf16[4,32,16,512]{3,2,0,1:T(8,128)(2,1)S(1)}, u32[]{:S(2)}, u32[]{:S(2)}) async-start(bf16[4,32,16,512]{3,2,0,1:T(8,128)(2,1)} %copy.17), calls=%async_computation | async-start | bytes 4194304 | tf_op jit(solution)/shard_map/all_to_all | solution.py:108
  61.7 25.5 %all-to-all-done = bf16[4,32,16,512]{3,2,0,1:T(8,128)(2,1)S(1)} async-done(((bf16[4,32,16,512]{3,2,0,1:T(8,128)(2,1)}), bf16[4,32,16,512]{3,2,0,1:T(8,128)(2,1)S(1)}, u32[]{:S(2)}, u32[]{:S(2)}) %all-to-all-start) | async-done | bytes 2097184 | tf_op jit(solution)/shard_map/all_to_all | solution.py:108
  99.1 583.7 %while.25 = (s32[]{:T(128)}, f32[16,16,2,16,256]{4,3,2,1,0:T(8,128)}, s32[16]{0:T(128)S(1)}, bf16[256,16,128]{2,1,0:T(8,128)(2,1)}, s32[128,256]{1,0:T(8,128)S(1...) while((s32[]{:T(128)}, f32[16,16,2,16,256]{4,3,2,1,0:T(8,128)}, ...), condition=%wide.region_4.5_spmd, body=%wide.region_3.4_spmd.sunk | while | flops 100925472 | bytes 3409779 | solution.py:82
  122.3 8.6 %fusion.90 = f32[16,16,256]{2,1,0:T(8,128)S(1)} fusion(s32[128,256]{1,0:T(8,128)S(1)} %get-tuple-element.322, s32[16]{0:T(128)S(1)} %add_add_fusion.2, bf16[256,16,128]{2,1,0:T(8,128)(2,1)} %get-tuple-element.321, s32[]{:T(128)S(6)} %select_n.88), kind=kOutput, calls=%fused_computation.44.clone.1 | convolution fusion | flops 25165824 | bytes 458820 | tf_op jit(solution)/shard_map/while/body/eval_jaxpr/kbc,kcm->kbm/dot_general | solution.py:72
  138.8 8.7 %fusion.88 = f32[16,16,256]{2,1,0:T(8,128)S(1)} fusion(s32[128,256]{1,0:T(8,128)S(1)} %get-tuple-element.322, s32[16]{0:T(128)S(1)} %add_add_fusion.2, bf16[256,16,128]{2,1,0:T(8,128)(2,1)} %get-tuple-element.321, s32[]{:T(128)S(6)} %select_n.88), kind=kOutput, calls=%fused_computation.45.clone.1 | convolution fusion | flops 25165824 | bytes 458820 | tf_op jit(solution)/shard_map/while/body/eval_jaxpr/kbc,kcm->kbm/dot_general | solution.py:76
  157.4 8.6 %fusion.90 = f32[16,16,256]{2,1,0:T(8,128)S(1)} fusion(s32[128,256]{1,0:T(8,128)S(1)} %get-tuple-element.322, s32[16]{0:T(128)S(1)} %add_add_fusion.2, bf16[256,16,128]{2,1,0:T(8,128)(2,1)} %get-tuple-element.321, s32[]{:T(128)S(6)} %select_n.88), kind=kOutput, calls=%fused_computation.44.clone.1 | convolution fusion | flops 25165824 | bytes 458820 | tf_op jit(solution)/shard_map/while/body/eval_jaxpr/kbc,kcm->kbm/dot_general | solution.py:72
  173.9 8.7 %fusion.88 = f32[16,16,256]{2,1,0:T(8,128)S(1)} fusion(s32[128,256]{1,0:T(8,128)S(1)} %get-tuple-element.322, s32[16]{0:T(128)S(1)} %add_add_fusion.2, bf16[256,16,128]{2,1,0:T(8,128)(2,1)} %get-tuple-element.321, s32[]{:T(128)S(6)} %select_n.88), kind=kOutput, calls=%fused_computation.45.clone.1 | convolution fusion | flops 25165824 | bytes 458820 | tf_op jit(solution)/shard_map/while/body/eval_jaxpr/kbc,kcm->kbm/dot_general | solution.py:76
  192.5 8.6 %fusion.90 = f32[16,16,256]{2,1,0:T(8,128)S(1)} fusion(s32[128,256]{1,0:T(8,128)S(1)} %get-tuple-element.322, s32[16]{0:T(128)S(1)} %add_add_fusion.2, bf16[256,16,128]{2,1,0:T(8,128)(2,1)} %get-tuple-element.321, s32[]{:T(128)S(6)} %select_n.88), kind=kOutput, calls=%fused_computation.44.clone.1 | convolution fusion | flops 25165824 | bytes 458820 | tf_op jit(solution)/shard_map/while/body/eval_jaxpr/kbc,kcm->kbm/dot_general | solution.py:72
  209.0 8.7 %fusion.88 = f32[16,16,256]{2,1,0:T(8,128)S(1)} fusion(s32[128,256]{1,0:T(8,128)S(1)} %get-tuple-element.322, s32[16]{0:T(128)S(1)} %add_add_fusion.2, bf16[256,16,128]{2,1,0:T(8,128)(2,1)} %get-tuple-element.321, s32[]{:T(128)S(6)} %select_n.88), kind=kOutput, calls=%fused_computation.45.clone.1 | convolution fusion | flops 25165824 | bytes 458820 | tf_op jit(solution)/shard_map/while/body/eval_jaxpr/kbc,kcm->kbm/dot_general | solution.py:76
  227.6 8.6 %fusion.90 = f32[16,16,256]{2,1,0:T(8,128)S(1)} fusion(s32[128,256]{1,0:T(8,128)S(1)} %get-tuple-element.322, s32[16]{0:T(128)S(1)} %add_add_fusion.2, bf16[256,16,128]{2,1,0:T(8,128)(2,1)} %get-tuple-element.321, s32[]{:T(128)S(6)} %select_n.88), kind=kOutput, calls=%fused_computation.44.clone.1 | convolution fusion | flops 25165824 | bytes 458820 | tf_op jit(solution)/shard_map/while/body/eval_jaxpr/kbc,kcm->kbm/dot_general | solution.py:72
  244.1 8.7 %fusion.88 = f32[16,16,256]{2,1,0:T(8,128)S(1)} fusion(s32[128,256]{1,0:T(8,128)S(1)} %get-tuple-element.322, s32[16]{0:T(128)S(1)} %add_add_fusion.2, bf16[256,16,128]{2,1,0:T(8,128)(2,1)} %get-tuple-element.321, s32[]{:T(128)S(6)} %select_n.88), kind=kOutput, calls=%fused_computation.45.clone.1 | convolution fusion | flops 25165824 | bytes 458820 | tf_op jit(solution)/shard_map/while/body/eval_jaxpr/kbc,kcm->kbm/dot_general | solution.py:76
  262.7 8.6 %fusion.90 = f32[16,16,256]{2,1,0:T(8,128)S(1)} fusion(s32[128,256]{1,0:T(8,128)S(1)} %get-tuple-element.322, s32[16]{0:T(128)S(1)} %add_add_fusion.2, bf16[256,16,128]{2,1,0:T(8,128)(2,1)} %get-tuple-element.321, s32[]{:T(128)S(6)} %select_n.88), kind=kOutput, calls=%fused_computation.44.clone.1 | convolution fusion | flops 25165824 | bytes 458820 | tf_op jit(solution)/shard_map/while/body/eval_jaxpr/kbc,kcm->kbm/dot_general | solution.py:72
  279.2 8.7 %fusion.88 = f32[16,16,256]{2,1,0:T(8,128)S(1)} fusion(s32[128,256]{1,0:T(8,128)S(1)} %get-tuple-element.322, s32[16]{0:T(128)S(1)} %add_add_fusion.2, bf16[256,16,128]{2,1,0:T(8,128)(2,1)} %get-tuple-element.321, s32[]{:T(128)S(6)} %select_n.88), kind=kOutput, calls=%fused_computation.45.clone.1 | convolution fusion | flops 25165824 | bytes 458820 | tf_op jit(solution)/shard_map/while/body/eval_jaxpr/kbc,kcm->kbm/dot_general | solution.py:76
  297.8 8.6 %fusion.90 = f32[16,16,256]{2,1,0:T(8,128)S(1)} fusion(s32[128,256]{1,0:T(8,128)S(1)} %get-tuple-element.322, s32[16]{0:T(128)S(1)} %add_add_fusion.2, bf16[256,16,128]{2,1,0:T(8,128)(2,1)} %get-tuple-element.321, s32[]{:T(128)S(6)} %select_n.88), kind=kOutput, calls=%fused_computation.44.clone.1 | convolution fusion | flops 25165824 | bytes 458820 | tf_op jit(solution)/shard_map/while/body/eval_jaxpr/kbc,kcm->kbm/dot_general | solution.py:72
  314.3 8.7 %fusion.88 = f32[16,16,256]{2,1,0:T(8,128)S(1)} fusion(s32[128,256]{1,0:T(8,128)S(1)} %get-tuple-element.322, s32[16]{0:T(128)S(1)} %add_add_fusion.2, bf16[256,16,128]{2,1,0:T(8,128)(2,1)} %get-tuple-element.321, s32[]{:T(128)S(6)} %select_n.88), kind=kOutput, calls=%fused_computation.45.clone.1 | convolution fusion | flops 25165824 | bytes 458820 | tf_op jit(solution)/shard_map/while/body/eval_jaxpr/kbc,kcm->kbm/dot_general | solution.py:76
  349.4 8.7 %fusion.88 = f32[16,16,256]{2,1,0:T(8,128)S(1)} fusion(s32[128,256]{1,0:T(8,128)S(1)} %get-tuple-element.322, s32[16]{0:T(128)S(1)} %add_add_fusion.2, bf16[256,16,128]{2,1,0:T(8,128)(2,1)} %get-tuple-element.321, s32[]{:T(128)S(6)} %select_n.88), kind=kOutput, calls=%fused_computation.45.clone.1 | convolution fusion | flops 25165824 | bytes 458820 | tf_op jit(solution)/shard_map/while/body/eval_jaxpr/kbc,kcm->kbm/dot_general | solution.py:76
  368.0 8.6 %fusion.90 = f32[16,16,256]{2,1,0:T(8,128)S(1)} fusion(s32[128,256]{1,0:T(8,128)S(1)} %get-tuple-element.322, s32[16]{0:T(128)S(1)} %add_add_fusion.2, bf16[256,16,128]{2,1,0:T(8,128)(2,1)} %get-tuple-element.321, s32[]{:T(128)S(6)} %select_n.88), kind=kOutput, calls=%fused_computation.44.clone.1 | convolution fusion | flops 25165824 | bytes 458820 | tf_op jit(solution)/shard_map/while/body/eval_jaxpr/kbc,kcm->kbm/dot_general | solution.py:72
  384.5 8.7 %fusion.88 = f32[16,16,256]{2,1,0:T(8,128)S(1)} fusion(s32[128,256]{1,0:T(8,128)S(1)} %get-tuple-element.322, s32[16]{0:T(128)S(1)} %add_add_fusion.2, bf16[256,16,128]{2,1,0:T(8,128)(2,1)} %get-tuple-element.321, s32[]{:T(128)S(6)} %select_n.88), kind=kOutput, calls=%fused_computation.45.clone.1 | convolution fusion | flops 25165824 | bytes 458820 | tf_op jit(solution)/shard_map/while/body/eval_jaxpr/kbc,kcm->kbm/dot_general | solution.py:76
  403.1 8.6 %fusion.90 = f32[16,16,256]{2,1,0:T(8,128)S(1)} fusion(s32[128,256]{1,0:T(8,128)S(1)} %get-tuple-element.322, s32[16]{0:T(128)S(1)} %add_add_fusion.2, bf16[256,16,128]{2,1,0:T(8,128)(2,1)} %get-tuple-element.321, s32[]{:T(128)S(6)} %select_n.88), kind=kOutput, calls=%fused_computation.44.clone.1 | convolution fusion | flops 25165824 | bytes 458820 | tf_op jit(solution)/shard_map/while/body/eval_jaxpr/kbc,kcm->kbm/dot_general | solution.py:72
  419.6 8.7 %fusion.88 = f32[16,16,256]{2,1,0:T(8,128)S(1)} fusion(s32[128,256]{1,0:T(8,128)S(1)} %get-tuple-element.322, s32[16]{0:T(128)S(1)} %add_add_fusion.2, bf16[256,16,128]{2,1,0:T(8,128)(2,1)} %get-tuple-element.321, s32[]{:T(128)S(6)} %select_n.88), kind=kOutput, calls=%fused_computation.45.clone.1 | convolution fusion | flops 25165824 | bytes 458820 | tf_op jit(solution)/shard_map/while/body/eval_jaxpr/kbc,kcm->kbm/dot_general | solution.py:76
  454.7 8.7 %fusion.88 = f32[16,16,256]{2,1,0:T(8,128)S(1)} fusion(s32[128,256]{1,0:T(8,128)S(1)} %get-tuple-element.322, s32[16]{0:T(128)S(1)} %add_add_fusion.2, bf16[256,16,128]{2,1,0:T(8,128)(2,1)} %get-tuple-element.321, s32[]{:T(128)S(6)} %select_n.88), kind=kOutput, calls=%fused_computation.45.clone.1 | convolution fusion | flops 25165824 | bytes 458820 | tf_op jit(solution)/shard_map/while/body/eval_jaxpr/kbc,kcm->kbm/dot_general | solution.py:76
  489.8 8.7 %fusion.88 = f32[16,16,256]{2,1,0:T(8,128)S(1)} fusion(s32[128,256]{1,0:T(8,128)S(1)} %get-tuple-element.322, s32[16]{0:T(128)S(1)} %add_add_fusion.2, bf16[256,16,128]{2,1,0:T(8,128)(2,1)} %get-tuple-element.321, s32[]{:T(128)S(6)} %select_n.88), kind=kOutput, calls=%fused_computation.45.clone.1 | convolution fusion | flops 25165824 | bytes 458820 | tf_op jit(solution)/shard_map/while/body/eval_jaxpr/kbc,kcm->kbm/dot_general | solution.py:76
  525.0 8.7 %fusion.88 = f32[16,16,256]{2,1,0:T(8,128)S(1)} fusion(s32[128,256]{1,0:T(8,128)S(1)} %get-tuple-element.322, s32[16]{0:T(128)S(1)} %add_add_fusion.2, bf16[256,16,128]{2,1,0:T(8,128)(2,1)} %get-tuple-element.321, s32[]{:T(128)S(6)} %select_n.88), kind=kOutput, calls=%fused_computation.45.clone.1 | convolution fusion | flops 25165824 | bytes 458820 | tf_op jit(solution)/shard_map/while/body/eval_jaxpr/kbc,kcm->kbm/dot_general | solution.py:76
  560.1 8.7 %fusion.88 = f32[16,16,256]{2,1,0:T(8,128)S(1)} fusion(s32[128,256]{1,0:T(8,128)S(1)} %get-tuple-element.322, s32[16]{0:T(128)S(1)} %add_add_fusion.2, bf16[256,16,128]{2,1,0:T(8,128)(2,1)} %get-tuple-element.321, s32[]{:T(128)S(6)} %select_n.88), kind=kOutput, calls=%fused_computation.45.clone.1 | convolution fusion | flops 25165824 | bytes 458820 | tf_op jit(solution)/shard_map/while/body/eval_jaxpr/kbc,kcm->kbm/dot_general | solution.py:76
  578.7 8.6 %fusion.90 = f32[16,16,256]{2,1,0:T(8,128)S(1)} fusion(s32[128,256]{1,0:T(8,128)S(1)} %get-tuple-element.322, s32[16]{0:T(128)S(1)} %add_add_fusion.2, bf16[256,16,128]{2,1,0:T(8,128)(2,1)} %get-tuple-element.321, s32[]{:T(128)S(6)} %select_n.88), kind=kOutput, calls=%fused_computation.44.clone.1 | convolution fusion | flops 25165824 | bytes 458820 | tf_op jit(solution)/shard_map/while/body/eval_jaxpr/kbc,kcm->kbm/dot_general | solution.py:72
  595.2 8.7 %fusion.88 = f32[16,16,256]{2,1,0:T(8,128)S(1)} fusion(s32[128,256]{1,0:T(8,128)S(1)} %get-tuple-element.322, s32[16]{0:T(128)S(1)} %add_add_fusion.2, bf16[256,16,128]{2,1,0:T(8,128)(2,1)} %get-tuple-element.321, s32[]{:T(128)S(6)} %select_n.88), kind=kOutput, calls=%fused_computation.45.clone.1 | convolution fusion | flops 25165824 | bytes 458820 | tf_op jit(solution)/shard_map/while/body/eval_jaxpr/kbc,kcm->kbm/dot_general | solution.py:76
  613.8 8.6 %fusion.90 = f32[16,16,256]{2,1,0:T(8,128)S(1)} fusion(s32[128,256]{1,0:T(8,128)S(1)} %get-tuple-element.322, s32[16]{0:T(128)S(1)} %add_add_fusion.2, bf16[256,16,128]{2,1,0:T(8,128)(2,1)} %get-tuple-element.321, s32[]{:T(128)S(6)} %select_n.88), kind=kOutput, calls=%fused_computation.44.clone.1 | convolution fusion | flops 25165824 | bytes 458820 | tf_op jit(solution)/shard_map/while/body/eval_jaxpr/kbc,kcm->kbm/dot_general | solution.py:72
  630.3 8.7 %fusion.88 = f32[16,16,256]{2,1,0:T(8,128)S(1)} fusion(s32[128,256]{1,0:T(8,128)S(1)} %get-tuple-element.322, s32[16]{0:T(128)S(1)} %add_add_fusion.2, bf16[256,16,128]{2,1,0:T(8,128)(2,1)} %get-tuple-element.321, s32[]{:T(128)S(6)} %select_n.88), kind=kOutput, calls=%fused_computation.45.clone.1 | convolution fusion | flops 25165824 | bytes 458820 | tf_op jit(solution)/shard_map/while/body/eval_jaxpr/kbc,kcm->kbm/dot_general | solution.py:76
  665.4 8.7 %fusion.88 = f32[16,16,256]{2,1,0:T(8,128)S(1)} fusion(s32[128,256]{1,0:T(8,128)S(1)} %get-tuple-element.322, s32[16]{0:T(128)S(1)} %add_add_fusion.2, bf16[256,16,128]{2,1,0:T(8,128)(2,1)} %get-tuple-element.321, s32[]{:T(128)S(6)} %select_n.88), kind=kOutput, calls=%fused_computation.45.clone.1 | convolution fusion | flops 25165824 | bytes 458820 | tf_op jit(solution)/shard_map/while/body/eval_jaxpr/kbc,kcm->kbm/dot_general | solution.py:76
  682.8 10.5 %copy.21 = f32[256,2,16,256]{0,2,1,3:T(8,128)} copy(f32[256,2,16,256]{3,2,1,0:T(8,128)} %bitcast.17) | data formatting | bytes 16777216 | tf_op jit(solution)/shard_map/reshape | solution.py:83
  693.3 78.6 %reduce-scatter.2.cloned.1.call-done = f32[256,2,16,64]{0,2,1,3:T(8,128)} async-done(((f32[256,2,16,256]{0,2,1,3:T(8,128)}), f32[256,2,16,64]{0,2,1,3:T(8,128)}) %reduce-scatter.2.cloned.1.call-update) | async-done | bytes 2097168 | tf_op jit(solution)/shard_map/reduce_scatter | solution.py:113
  (134 shorter events, 381.6 us)
Async XLA Ops:
  47.6 11.4 %copy-start = (s32[256,512]{1,0:T(8,128)S(1)}, s32[256,512]{1,0:T(8,128)}, u32[]{:S(2)}) copy-start(s32[256,512]{1,0:T(8,128)} %param.9) | copy-start | bytes 1572868
  47.6 39.6 %all-to-all-start = ((bf16[4,32,16,512]{3,2,0,1:T(8,128)(2,1)}), bf16[4,32,16,512]{3,2,0,1:T(8,128)(2,1)S(1)}, u32[]{:S(2)}, u32[]{:S(2)}) async-start(bf16[4,32,16,512]{3,2,0,1:T(8,128)(2,1)} %copy.17), calls=%async_computation | async-start | bytes 4194304 | tf_op jit(solution)/shard_map/all_to_all | solution.py:108
  58.9 712.9 %reduce-scatter.2.cloned.1.call-start = ((), (), s32[]{:S(2)}) async-start(), calls=%async_computation.2 | async-start | bytes 10485760 | tf_op jit(solution)/shard_map/reduce_scatter | solution.py:113
Sparse Core Ops, SparseCore 0:
  693.4 78.4 reduce-scatter.1
where the time goes:
time: 791 us; the launch traced here: 782 us
  matrix products  545 us (69%)
  waiting for transfers between devices  104 us (13%)
  other arithmetic  37.2 us (5%)
  local copies, waits for them, and re-layouts  35.7 us (5%)
  loops' own time  35.1 us (4%)
  between operations  13.9 us (2%)
  starting transfers between devices  11.4 us (1%)
    dot_general x16, matrix products, one_block(): jnp.einsum('kbc,kcm->kbm', real_piece, sine, preferred_element_type=jnp.f...  139 us
    dot_general x16, matrix products, one_block(): jnp.einsum('kbc,kcm->kbm', real_piece, cosine, preferred_element_type=jnp...  138 us
    dot_general x16, matrix products, one_block(): jnp.einsum('kbc,kcm->kbm', imag_piece, sine, preferred_element_type=jnp.f...  126 us
    dot_general x16, matrix products, one_block(): jnp.einsum('kbc,kcm->kbm', imag_piece, cosine, preferred_element_type=jnp...  125 us
    reduce_scatter x1, waiting for transfers between devices, body(): lax.psum_scatter(partial_spec, 'grp', scatter_dimension=3, tiled=True)  78.6 us
    another operation x1, loops' own time, dedisperse(): blocks = lax.map(one_block, jnp.arange(bins_count // KBLK, dtype=jnp.int32))  32.2 us
    all_to_all x1, waiting for transfers between devices, body(): lax.all_to_all(blocked, 'chan', split_axis=1, concat_axis=0, tiled=True)  25.5 us
  transfers between devices with their start and end apart: 2, of which 2 were waited for; matrix products, arithmetic and copies ran while one was open for 0% of the time, Pallas kernels for 0%

commit v1 on v0

--- a/solution.py
+++ b/solution.py
@@ -8,6 +8,19 @@
 INTEG = 8
 PHASES = 4096
 KBLK = 16
+
+
+def clear_gates_on(patch, axis_id):
+    w_next = jnp.concatenate(
+        lax.all_to_all(
+            jnp.stack(jnp.split(patch, lax.axis_size(axis_id), axis=1)),
+            axis_id,
+            split_axis=0,
+            concat_axis=0,
+        ),
+        axis=0,
+    )
+    return w_next
 
 
 def beam_matrix(delays, channel, channel_count):
@@ -104,11 +117,7 @@
     beam_total = detected.shape[1]
     blocked = detected.reshape(chan_local, chan_count, beam_total // chan_count, detected.shape[2])
     partial_spec = dedisperse(
-        spectra(
-            lax.all_to_all(blocked, "chan", split_axis=1, concat_axis=0, tiled=True)[:, 0], table
-        ),
-        selected,
-        phase_scale,
+        spectra(clear_gates_on(blocked, "chan")[:, 0], table), selected, phase_scale
     )
     summed = lax.psum_scatter(partial_spec, "grp", scatter_dimension=3, tiled=True)
     result = summed[:, 0] ** 2 + summed[:, 1] ** 2

time: 791 us -> 809 us (1.023)
  local copies, waits for them, and re-layouts: 35.7 us -> 54.1 us
    unnamed x3 -> x34, local copies, waits for them, and re-layouts: 0.2 us -> 19.5 us
where the time goes in v1:
time: 809 us; the launch traced here: 800 us
  matrix products  545 us (67%)
  waiting for transfers between devices  104 us (13%)
  local copies, waits for them, and re-layouts  54.1 us (7%)
  other arithmetic  37.2 us (5%)
  loops' own time  35.1 us (4%)
  between operations  13.9 us (2%)
  starting transfers between devices  11.4 us (1%)
    dot_general x16, matrix products, one_block(): jnp.einsum('kbc,kcm->kbm', real_piece, sine, preferred_element_type=jnp.f...  139 us
    dot_general x16, matrix products, one_block(): jnp.einsum('kbc,kcm->kbm', real_piece, cosine, preferred_element_type=jnp...  138 us
    dot_general x16, matrix products, one_block(): jnp.einsum('kbc,kcm->kbm', imag_piece, sine, preferred_element_type=jnp.f...  126 us
    dot_general x16, matrix products, one_block(): jnp.einsum('kbc,kcm->kbm', imag_piece, cosine, preferred_element_type=jnp...  125 us
    reduce_scatter x1, waiting for transfers between devices, body(): lax.psum_scatter(partial_spec, 'grp', scatter_dimension=3, tiled=True)  78.6 us
    another operation x1, loops' own time, dedisperse(): blocks = lax.map(one_block, jnp.arange(bins_count // KBLK, dtype=jnp.int32))  32.2 us
    all_to_all x1, waiting for transfers between devices, clear_gates_on(): lax.all_to_all(jnp.stack(jnp.split(patch, lax.axis_size(axis_id), axis=1)...  25.5 us
    unnamed x34, local copies, waits for them, and re-layouts  19.5 us
  transfers between devices with their start and end apart: 2, of which 2 were waited for; matrix products, arithmetic and copies ran while one was open for 0% of the time, Pallas kernels for 0%

profile of v1, /device:TPU:1, one launch (start us, length us, event | category | flops | bytes accessed | tf_op | source)
XLA Modules:
  0.0 800.2 jit_solution(8520197458898960704)
XLA Ops:
  6.5 39.4 %while.24 = (s32[]{:T(128)}, bf16[4,512,512]{2,1,0:T(8,128)(2,1)S(1)}, bf16[4,4096,128]{2,1,0:T(8,128)(2,1)}, s32[4]{0:T(128)S(1)}, s32[]{:T(128)}, /*index=5*/s32[64,512]{1,0:T(8,128)}, s32[]{:T(128)}, s32[]{:T(128)}) while((s32[]{:T(128)}, bf16[4,512,512]{2,1,0:T(8,128)(2,1)S(1)}, bf16[4,4096,128]{2,1,0:T(8,128)(2,1)}, s32[4]{0:T(128)S(1)}, ...), condition=%wide.region_2.3_spmd, body=%wide.region_0.2_spmd.sunk | while | flops 1084129280 | bytes 39846528 | solution.py:110
  66.0 11.3 %all-to-all-start = ((bf16[32,4,1,16,512]{4,3,1,2,0:T(8,128)(2,1)}), bf16[32,4,1,16,512]{4,3,1,2,0:T(8,128)(2,1)S(1)}, u32[]{:S(2)}, u32[]{:S(2)}) async-start(bf16[32,4,1,16,512]{4,3,1,2,0:T(8,128)(2,1)} %constant_dynamic-update-slice_fusion.1), calls=%async_computation | async-start | bytes 4194304 | tf_op jit(solution)/shard_map/all_to_all | solution.py:15
  80.1 25.5 %all-to-all-done = bf16[32,4,1,16,512]{4,3,1,2,0:T(8,128)(2,1)S(1)} async-done(((bf16[32,4,1,16,512]{4,3,1,2,0:T(8,128)(2,1)}), bf16[32,4,1,16,512]{4,3,1,2,0:T(8,128)(2,1)S(1)}, u32[]{:S(2)}, u32[]{:S(2)}) %all-to-all-start) | async-done | bytes 2097184 | tf_op jit(solution)/shard_map/all_to_all | solution.py:15
  117.5 583.7 %while.25 = (s32[]{:T(128)}, f32[16,16,2,16,256]{4,3,2,1,0:T(8,128)}, s32[16]{0:T(128)S(1)}, bf16[256,16,128]{2,1,0:T(8,128)(2,1)}, s32[128,256]{1,0:T(8,128)S(1...) while((s32[]{:T(128)}, f32[16,16,2,16,256]{4,3,2,1,0:T(8,128)}, ...), condition=%wide.region_4.5_spmd, body=%wide.region_3.4_spmd.sunk | while | flops 100925472 | bytes 3409779 | solution.py:95
  140.6 8.6 %fusion.90 = f32[16,16,256]{2,1,0:T(8,128)S(1)} fusion(s32[128,256]{1,0:T(8,128)S(1)} %get-tuple-element.322, s32[16]{0:T(128)S(1)} %add_add_fusion.2, bf16[256,16,128]{2,1,0:T(8,128)(2,1)} %get-tuple-element.321, s32[]{:T(128)S(6)} %select_n.88), kind=kOutput, calls=%fused_computation.44.clone.1 | convolution fusion | flops 25165824 | bytes 458820 | tf_op jit(solution)/shard_map/while/body/eval_jaxpr/kbc,kcm->kbm/dot_general | solution.py:85
  157.1 8.7 %fusion.88 = f32[16,16,256]{2,1,0:T(8,128)S(1)} fusion(s32[128,256]{1,0:T(8,128)S(1)} %get-tuple-element.322, s32[16]{0:T(128)S(1)} %add_add_fusion.2, bf16[256,16,128]{2,1,0:T(8,128)(2,1)} %get-tuple-element.321, s32[]{:T(128)S(6)} %select_n.88), kind=kOutput, calls=%fused_computation.45.clone.1 | convolution fusion | flops 25165824 | bytes 458820 | tf_op jit(solution)/shard_map/while/body/eval_jaxpr/kbc,kcm->kbm/dot_general | solution.py:89
  175.7 8.6 %fusion.90 = f32[16,16,256]{2,1,0:T(8,128)S(1)} fusion(s32[128,256]{1,0:T(8,128)S(1)} %get-tuple-element.322, s32[16]{0:T(128)S(1)} %add_add_fusion.2, bf16[256,16,128]{2,1,0:T(8,128)(2,1)} %get-tuple-element.321, s32[]{:T(128)S(6)} %select_n.88), kind=kOutput, calls=%fused_computation.44.clone.1 | convolution fusion | flops 25165824 | bytes 458820 | tf_op jit(solution)/shard_map/while/body/eval_jaxpr/kbc,kcm->kbm/dot_general | solution.py:85
  192.2 8.7 %fusion.88 = f32[16,16,256]{2,1,0:T(8,128)S(1)} fusion(s32[128,256]{1,0:T(8,128)S(1)} %get-tuple-element.322, s32[16]{0:T(128)S(1)} %add_add_fusion.2, bf16[256,16,128]{2,1,0:T(8,128)(2,1)} %get-tuple-element.321, s32[]{:T(128)S(6)} %select_n.88), kind=kOutput, calls=%fused_computation.45.clone.1 | convolution fusion | flops 25165824 | bytes 458820 | tf_op jit(solution)/shard_map/while/body/eval_jaxpr/kbc,kcm->kbm/dot_general | solution.py:89
  210.8 8.6 %fusion.90 = f32[16,16,256]{2,1,0:T(8,128)S(1)} fusion(s32[128,256]{1,0:T(8,128)S(1)} %get-tuple-element.322, s32[16]{0:T(128)S(1)} %add_add_fusion.2, bf16[256,16,128]{2,1,0:T(8,128)(2,1)} %get-tuple-element.321, s32[]{:T(128)S(6)} %select_n.88), kind=kOutput, calls=%fused_computation.44.clone.1 | convolution fusion | flops 25165824 | bytes 458820 | tf_op jit(solution)/shard_map/while/body/eval_jaxpr/kbc,kcm->kbm/dot_general | solution.py:85
  227.3 8.7 %fusion.88 = f32[16,16,256]{2,1,0:T(8,128)S(1)} fusion(s32[128,256]{1,0:T(8,128)S(1)} %get-tuple-element.322, s32[16]{0:T(128)S(1)} %add_add_fusion.2, bf16[256,16,128]{2,1,0:T(8,128)(2,1)} %get-tuple-element.321, s32[]{:T(128)S(6)} %select_n.88), kind=kOutput, calls=%fused_computation.45.clone.1 | convolution fusion | flops 25165824 | bytes 458820 | tf_op jit(solution)/shard_map/while/body/eval_jaxpr/kbc,kcm->kbm/dot_general | solution.py:89
  246.0 8.6 %fusion.90 = f32[16,16,256]{2,1,0:T(8,128)S(1)} fusion(s32[128,256]{1,0:T(8,128)S(1)} %get-tuple-element.322, s32[16]{0:T(128)S(1)} %add_add_fusion.2, bf16[256,16,128]{2,1,0:T(8,128)(2,1)} %get-tuple-element.321, s32[]{:T(128)S(6)} %select_n.88), kind=kOutput, calls=%fused_computation.44.clone.1 | convolution fusion | flops 25165824 | bytes 458820 | tf_op jit(solution)/shard_map/while/body/eval_jaxpr/kbc,kcm->kbm/dot_general | solution.py:85
  262.5 8.7 %fusion.88 = f32[16,16,256]{2,1,0:T(8,128)S(1)} fusion(s32[128,256]{1,0:T(8,128)S(1)} %get-tuple-element.322, s32[16]{0:T(128)S(1)} %add_add_fusion.2, bf16[256,16,128]{2,1,0:T(8,128)(2,1)} %get-tuple-element.321, s32[]{:T(128)S(6)} %select_n.88), kind=kOutput, calls=%fused_computation.45.clone.1 | convolution fusion | flops 25165824 | bytes 458820 | tf_op jit(solution)/shard_map/while/body/eval_jaxpr/kbc,kcm->kbm/dot_general | solution.py:89
  281.1 8.6 %fusion.90 = f32[16,16,256]{2,1,0:T(8,128)S(1)} fusion(s32[128,256]{1,0:T(8,128)S(1)} %get-tuple-element.322, s32[16]{0:T(128)S(1)} %add_add_fusion.2, bf16[256,16,128]{2,1,0:T(8,128)(2,1)} %get-tuple-element.321, s32[]{:T(128)S(6)} %select_n.88), kind=kOutput, calls=%fused_computation.44.clone.1 | convolution fusion | flops 25165824 | bytes 458820 | tf_op jit(solution)/shard_map/while/body/eval_jaxpr/kbc,kcm->kbm/dot_general | solution.py:85
  297.6 8.7 %fusion.88 = f32[16,16,256]{2,1,0:T(8,128)S(1)} fusion(s32[128,256]{1,0:T(8,128)S(1)} %get-tuple-element.322, s32[16]{0:T(128)S(1)} %add_add_fusion.2, bf16[256,16,128]{2,1,0:T(8,128)(2,1)} %get-tuple-element.321, s32[]{:T(128)S(6)} %select_n.88), kind=kOutput, calls=%fused_computation.45.clone.1 | convolution fusion | flops 25165824 | bytes 458820 | tf_op jit(solution)/shard_map/while/body/eval_jaxpr/kbc,kcm->kbm/dot_general | solution.py:89
  316.2 8.6 %fusion.90 = f32[16,16,256]{2,1,0:T(8,128)S(1)} fusion(s32[128,256]{1,0:T(8,128)S(1)} %get-tuple-element.322, s32[16]{0:T(128)S(1)} %add_add_fusion.2, bf16[256,16,128]{2,1,0:T(8,128)(2,1)} %get-tuple-element.321, s32[]{:T(128)S(6)} %select_n.88), kind=kOutput, calls=%fused_computation.44.clone.1 | convolution fusion | flops 25165824 | bytes 458820 | tf_op jit(solution)/shard_map/while/body/eval_jaxpr/kbc,kcm->kbm/dot_general | solution.py:85
  332.7 8.7 %fusion.88 = f32[16,16,256]{2,1,0:T(8,128)S(1)} fusion(s32[128,256]{1,0:T(8,128)S(1)} %get-tuple-element.322, s32[16]{0:T(128)S(1)} %add_add_fusion.2, bf16[256,16,128]{2,1,0:T(8,128)(2,1)} %get-tuple-element.321, s32[]{:T(128)S(6)} %select_n.88), kind=kOutput, calls=%fused_computation.45.clone.1 | convolution fusion | flops 25165824 | bytes 458820 | tf_op jit(solution)/shard_map/while/body/eval_jaxpr/kbc,kcm->kbm/dot_general | solution.py:89
  351.3 8.6 %fusion.90 = f32[16,16,256]{2,1,0:T(8,128)S(1)} fusion(s32[128,256]{1,0:T(8,128)S(1)} %get-tuple-element.322, s32[16]{0:T(128)S(1)} %add_add_fusion.2, bf16[256,16,128]{2,1,0:T(8,128)(2,1)} %get-tuple-element.321, s32[]{:T(128)S(6)} %select_n.88), kind=kOutput, calls=%fused_computation.44.clone.1 | convolution fusion | flops 25165824 | bytes 458820 | tf_op jit(solution)/shard_map/while/body/eval_jaxpr/kbc,kcm->kbm/dot_general | solution.py:85
  367.8 8.7 %fusion.88 = f32[16,16,256]{2,1,0:T(8,128)S(1)} fusion(s32[128,256]{1,0:T(8,128)S(1)} %get-tuple-element.322, s32[16]{0:T(128)S(1)} %add_add_fusion.2, bf16[256,16,128]{2,1,0:T(8,128)(2,1)} %get-tuple-element.321, s32[]{:T(128)S(6)} %select_n.88), kind=kOutput, calls=%fused_computation.45.clone.1 | convolution fusion | flops 25165824 | bytes 458820 | tf_op jit(solution)/shard_map/while/body/eval_jaxpr/kbc,kcm->kbm/dot_general | solution.py:89
  386.4 8.6 %fusion.90 = f32[16,16,256]{2,1,0:T(8,128)S(1)} fusion(s32[128,256]{1,0:T(8,128)S(1)} %get-tuple-element.322, s32[16]{0:T(128)S(1)} %add_add_fusion.2, bf16[256,16,128]{2,1,0:T(8,128)(2,1)} %get-tuple-element.321, s32[]{:T(128)S(6)} %select_n.88), kind=kOutput, calls=%fused_computation.44.clone.1 | convolution fusion | flops 25165824 | bytes 458820 | tf_op jit(solution)/shard_map/while/body/eval_jaxpr/kbc,kcm->kbm/dot_general | solution.py:85
  402.9 8.7 %fusion.88 = f32[16,16,256]{2,1,0:T(8,128)S(1)} fusion(s32[128,256]{1,0:T(8,128)S(1)} %get-tuple-element.322, s32[16]{0:T(128)S(1)} %add_add_fusion.2, bf16[256,16,128]{2,1,0:T(8,128)(2,1)} %get-tuple-element.321, s32[]{:T(128)S(6)} %select_n.88), kind=kOutput, calls=%fused_computation.45.clone.1 | convolution fusion | flops 25165824 | bytes 458820 | tf_op jit(solution)/shard_map/while/body/eval_jaxpr/kbc,kcm->kbm/dot_general | solution.py:89
  438.0 8.7 %fusion.88 = f32[16,16,256]{2,1,0:T(8,128)S(1)} fusion(s32[128,256]{1,0:T(8,128)S(1)} %get-tuple-element.322, s32[16]{0:T(128)S(1)} %add_add_fusion.2, bf16[256,16,128]{2,1,0:T(8,128)(2,1)} %get-tuple-element.321, s32[]{:T(128)S(6)} %select_n.88), kind=kOutput, calls=%fused_computation.45.clone.1 | convolution fusion | flops 25165824 | bytes 458820 | tf_op jit(solution)/shard_map/while/body/eval_jaxpr/kbc,kcm->kbm/dot_general | solution.py:89
  473.1 8.7 %fusion.88 = f32[16,16,256]{2,1,0:T(8,128)S(1)} fusion(s32[128,256]{1,0:T(8,128)S(1)} %get-tuple-element.322, s32[16]{0:T(128)S(1)} %add_add_fusion.2, bf16[256,16,128]{2,1,0:T(8,128)(2,1)} %get-tuple-element.321, s32[]{:T(128)S(6)} %select_n.88), kind=kOutput, calls=%fused_computation.45.clone.1 | convolution fusion | flops 25165824 | bytes 458820 | tf_op jit(solution)/shard_map/while/body/eval_jaxpr/kbc,kcm->kbm/dot_general | solution.py:89
  491.7 8.6 %fusion.90 = f32[16,16,256]{2,1,0:T(8,128)S(1)} fusion(s32[128,256]{1,0:T(8,128)S(1)} %get-tuple-element.322, s32[16]{0:T(128)S(1)} %add_add_fusion.2, bf16[256,16,128]{2,1,0:T(8,128)(2,1)} %get-tuple-element.321, s32[]{:T(128)S(6)} %select_n.88), kind=kOutput, calls=%fused_computation.44.clone.1 | convolution fusion | flops 25165824 | bytes 458820 | tf_op jit(solution)/shard_map/while/body/eval_jaxpr/kbc,kcm->kbm/dot_general | solution.py:85
  508.2 8.7 %fusion.88 = f32[16,16,256]{2,1,0:T(8,128)S(1)} fusion(s32[128,256]{1,0:T(8,128)S(1)} %get-tuple-element.322, s32[16]{0:T(128)S(1)} %add_add_fusion.2, bf16[256,16,128]{2,1,0:T(8,128)(2,1)} %get-tuple-element.321, s32[]{:T(128)S(6)} %select_n.88), kind=kOutput, calls=%fused_computation.45.clone.1 | convolution fusion | flops 25165824 | bytes 458820 | tf_op jit(solution)/shard_map/while/body/eval_jaxpr/kbc,kcm->kbm/dot_general | solution.py:89
  526.9 8.6 %fusion.90 = f32[16,16,256]{2,1,0:T(8,128)S(1)} fusion(s32[128,256]{1,0:T(8,128)S(1)} %get-tuple-element.322, s32[16]{0:T(128)S(1)} %add_add_fusion.2, bf16[256,16,128]{2,1,0:T(8,128)(2,1)} %get-tuple-element.321, s32[]{:T(128)S(6)} %select_n.88), kind=kOutput, calls=%fused_computation.44.clone.1 | convolution fusion | flops 25165824 | bytes 458820 | tf_op jit(solution)/shard_map/while/body/eval_jaxpr/kbc,kcm->kbm/dot_general | solution.py:85
  543.3 8.7 %fusion.88 = f32[16,16,256]{2,1,0:T(8,128)S(1)} fusion(s32[128,256]{1,0:T(8,128)S(1)} %get-tuple-element.322, s32[16]{0:T(128)S(1)} %add_add_fusion.2, bf16[256,16,128]{2,1,0:T(8,128)(2,1)} %get-tuple-element.321, s32[]{:T(128)S(6)} %select_n.88), kind=kOutput, calls=%fused_computation.45.clone.1 | convolution fusion | flops 25165824 | bytes 458820 | tf_op jit(solution)/shard_map/while/body/eval_jaxpr/kbc,kcm->kbm/dot_general | solution.py:89
  578.4 8.7 %fusion.88 = f32[16,16,256]{2,1,0:T(8,128)S(1)} fusion(s32[128,256]{1,0:T(8,128)S(1)} %get-tuple-element.322, s32[16]{0:T(128)S(1)} %add_add_fusion.2, bf16[256,16,128]{2,1,0:T(8,128)(2,1)} %get-tuple-element.321, s32[]{:T(128)S(6)} %select_n.88), kind=kOutput, calls=%fused_computation.45.clone.1 | convolution fusion | flops 25165824 | bytes 458820 | tf_op jit(solution)/shard_map/while/body/eval_jaxpr/kbc,kcm->kbm/dot_general | solution.py:89
  613.5 8.7 %fusion.88 = f32[16,16,256]{2,1,0:T(8,128)S(1)} fusion(s32[128,256]{1,0:T(8,128)S(1)} %get-tuple-element.322, s32[16]{0:T(128)S(1)} %add_add_fusion.2, bf16[256,16,128]{2,1,0:T(8,128)(2,1)} %get-tuple-element.321, s32[]{:T(128)S(6)} %select_n.88), kind=kOutput, calls=%fused_computation.45.clone.1 | convolution fusion | flops 25165824 | bytes 458820 | tf_op jit(solution)/shard_map/while/body/eval_jaxpr/kbc,kcm->kbm/dot_general | solution.py:89
  648.7 8.7 %fusion.88 = f32[16,16,256]{2,1,0:T(8,128)S(1)} fusion(s32[128,256]{1,0:T(8,128)S(1)} %get-tuple-element.322, s32[16]{0:T(128)S(1)} %add_add_fusion.2, bf16[256,16,128]{2,1,0:T(8,128)(2,1)} %get-tuple-element.321, s32[]{:T(128)S(6)} %select_n.88), kind=kOutput, calls=%fused_computation.45.clone.1 | convolution fusion | flops 25165824 | bytes 458820 | tf_op jit(solution)/shard_map/while/body/eval_jaxpr/kbc,kcm->kbm/dot_general | solution.py:89
  683.7 8.7 %fusion.88 = f32[16,16,256]{2,1,0:T(8,128)S(1)} fusion(s32[128,256]{1,0:T(8,128)S(1)} %get-tuple-element.322, s32[16]{0:T(128)S(1)} %add_add_fusion.2, bf16[256,16,128]{2,1,0:T(8,128)(2,1)} %get-tuple-element.321, s32[]{:T(128)S(6)} %select_n.88), kind=kOutput, calls=%fused_computation.45.clone.1 | convolution fusion | flops 25165824 | bytes 458820 | tf_op jit(solution)/shard_map/while/body/eval_jaxpr/kbc,kcm->kbm/dot_general | solution.py:89
  701.1 10.5 %copy.142 = f32[256,2,16,256]{0,2,1,3:T(8,128)} copy(f32[256,2,16,256]{3,2,1,0:T(8,128)} %bitcast.47) | data formatting | bytes 16777216 | tf_op jit(solution)/shard_map/reshape | solution.py:96
  711.6 78.6 %reduce-scatter.2.cloned.1.call-done = f32[256,2,16,64]{0,2,1,3:T(8,128)} async-done(((f32[256,2,16,256]{0,2,1,3:T(8,128)}), f32[256,2,16,64]{0,2,1,3:T(8,128)}) %reduce-scatter.2.cloned.1.call-update) | async-done | bytes 2097168 | tf_op jit(solution)/shard_map/reduce_scatter | solution.py:122
  (165 shorter events, 400.0 us)
Async XLA Ops:
  66.0 11.4 %copy-start = (s32[256,512]{1,0:T(8,128)S(1)}, s32[256,512]{1,0:T(8,128)}, u32[]{:S(2)}) copy-start(s32[256,512]{1,0:T(8,128)} %param.9) | copy-start | bytes 1572868
  66.0 39.6 %all-to-all-start = ((bf16[32,4,1,16,512]{4,3,1,2,0:T(8,128)(2,1)}), bf16[32,4,1,16,512]{4,3,1,2,0:T(8,128)(2,1)S(1)}, u32[]{:S(2)}, u32[]{:S(2)}) async-start(bf16[32,4,1,16,512]{4,3,1,2,0:T(8,128)(2,1)} %constant_dynamic-update-slice_fusion.1), calls=%async_computation | async-start | bytes 4194304 | tf_op jit(solution)/shard_map/all_to_all | solution.py:15
  77.3 712.9 %reduce-scatter.2.cloned.1.call-start = ((), (), s32[]{:S(2)}) async-start(), calls=%async_computation.2 | async-start | bytes 10485760 | tf_op jit(solution)/shard_map/reduce_scatter | solution.py:122
Sparse Core Ops, SparseCore 0:
  711.8 78.4 reduce-scatter.1
